TPU v7x, 256 devices: a whole 4x4x8 slice. The times are simulated.
256 devices in a mesh: group: 32 (over x, z), members: 8 (over y, core).
Axes of the slice: x: 4, y: 4, z: 8, core: 2. Of those that a mesh axis runs over, the one named last changes fastest.
Arguments:
- out_grad: bfloat16 [32768, 3584], P(('group', 'members')), may hold values from -4 to 4
- hidden_act: bfloat16 [32768, 4, 1024], P(('group', 'members')), may hold values from -0.23925781 to 0.23925781
- gate_weight: bfloat16 [32768, 4], P(('group', 'members')), may hold values from 0.099609375 to 2.5
- routes: int32 [32768, 4], P(('group', 'members')), may hold values from 0 to 127, all different within a row; in each aligned block of 128 rows (0 to 127, 128 to 255, ...) at most 7 rows name the same one
- down_weight: bfloat16 [256, 1024, 1792], P(('group', 'members')), may hold values from -0.1875 to 0.1875
Outputs:
- weight_grad: bfloat16 [256, 1024, 1792], P(('group', 'members'))
- hidden_grad: bfloat16 [32768, 4, 1024], P(('group', 'members'))
- gate_grad: float32 [32768, 4], P(('group', 'members'))
Inputs may be any that keep to these rules, and one draw needn't show every extreme that they name: `routes`: each row names 4 different experts. Within the rows of one device no expert is named more than 7 times, and in some device's rows some expert is named exactly 7 times.
All inputs are finite; a program needn't handle non-finite values.
Results may differ from a plain program's by a relative error of at most 0.0085.
Values may be sent and summed in bfloat16 or wider, within the bound.
A program may use at most 128 MiB of HBM per device.

v0:
```python
import jax
import jax.numpy as jnp
from jax import lax
from jax.sharding import PartitionSpec as P


def local(out_grad, hidden_act, gate_weight, routes, down_weight):
    groups = lax.axis_size("group")
    members = lax.axis_size("members")
    tok_rows, model_width = out_grad.shape
    routes_each = routes.shape[1]
    hidden_units = hidden_act.shape[2]
    experts = groups * members // 2
    half_width = model_width // 2
    capacity = max(2, 7 * tok_rows * routes_each // (4 * experts))
    slot_count = tok_rows * routes_each
    row_count = groups * members * capacity
    targets = routes.reshape(slot_count)
    onehot = (targets[:, None] == jnp.arange(experts, dtype=jnp.int32)[None, :]).astype(jnp.int32)
    positions = jnp.sum(jnp.cumsum(onehot, axis=0) * onehot, axis=1) - 1
    grad_rows = jnp.repeat(out_grad, routes_each, axis=0)
    grad_buffer = jnp.zeros((experts, 2, capacity, half_width), jnp.bfloat16)
    grad_buffer = grad_buffer.at[targets, :, positions].set(
        grad_rows.reshape(slot_count, 2, half_width)
    )
    gate_values = gate_weight.reshape(slot_count)
    gate_buffer = jnp.zeros((experts, 2, capacity), jnp.bfloat16)
    gate_buffer = gate_buffer.at[targets, :, positions].set(
        jnp.broadcast_to(gate_values[:, None], (slot_count, 2))
    )
    hidden = hidden_act.reshape(slot_count, hidden_units)
    hidden_buffer = jnp.zeros((experts, 2, capacity, hidden_units), jnp.bfloat16)
    hidden_buffer = hidden_buffer.at[targets, :, positions].set(
        jnp.broadcast_to(hidden[:, None, :], (slot_count, 2, hidden_units))
    )
    grad_in, hidden_in, gate_in = (
        lax.all_to_all(
            lax.all_to_all(
                grad_buffer.reshape(groups, members, capacity, half_width),
                "group",
                split_axis=0,
                concat_axis=0,
                tiled=True,
            ),
            "members",
            split_axis=1,
            concat_axis=1,
            tiled=True,
        ),
        lax.all_to_all(
            lax.all_to_all(
                hidden_buffer.reshape(groups, members, capacity, hidden_buffer.shape[3]),
                "group",
                split_axis=0,
                concat_axis=0,
                tiled=True,
            ),
            "members",
            split_axis=1,
            concat_axis=1,
            tiled=True,
        ),
        lax.all_to_all(
            lax.all_to_all(
                gate_buffer.reshape(groups, members, capacity),
                "group",
                split_axis=0,
                concat_axis=0,
                tiled=True,
            ),
            "members",
            split_axis=1,
            concat_axis=1,
            tiled=True,
        ),
    )
    grad_in = grad_in.reshape(row_count, half_width)
    gate_in = gate_in.reshape(row_count)
    hidden_full = hidden_in.reshape(row_count, hidden_units)
    weight = down_weight[0]
    partial_value = lax.dot_general(
        grad_in, weight, (((1,), (1,)), ((), ())), preferred_element_type=jnp.float32
    )
    scaled = (gate_in.astype(jnp.float32)[:, None] * grad_in.astype(jnp.float32)).astype(
        jnp.bfloat16
    )
    weight_grad = lax.dot_general(
        hidden_full, scaled, (((0,), (0,)), ((), ())), preferred_element_type=jnp.float32
    ).astype(jnp.bfloat16)[None]
    returned = lax.all_to_all(
        lax.all_to_all(
            partial_value.reshape(groups, members, capacity, hidden_units),
            "members",
            split_axis=1,
            concat_axis=1,
            tiled=True,
        ),
        "group",
        split_axis=0,
        concat_axis=0,
        tiled=True,
    )
    picked = returned.reshape(experts, 2, capacity, hidden_units)[targets, :, positions]
    unscaled = (picked[:, 0] + picked[:, 1]).astype(jnp.bfloat16)
    unscaled_wide = unscaled.astype(jnp.float32)
    hidden_grad = (
        (gate_values.astype(jnp.float32)[:, None] * unscaled_wide)
        .astype(jnp.bfloat16)
        .reshape(tok_rows, routes_each, hidden_units)
    )
    gate_grad = jnp.sum(unscaled_wide * hidden.astype(jnp.float32), axis=1).reshape(
        tok_rows, routes_each
    )
    return (weight_grad, hidden_grad, gate_grad)


def solution(mesh):
    return jax.shard_map(
        local,
        mesh=mesh,
        in_specs=(
            P(("group", "members"), None),
            P(("group", "members"), None, None),
            P(("group", "members"), None),
            P(("group", "members"), None),
            P(("group", "members"), None, None),
        ),
        out_specs=(
            P(("group", "members"), None, None),
            P(("group", "members"), None, None),
            P(("group", "members"), None),
        ),
        check_vma=False,
    )
```

profile of v0, /device:TPU:5, one launch (start us, length us, event | category | flops | bytes accessed | tf_op | source)
XLA Modules:
  0.0 861.7 jit_solution(13757305403740825294)
XLA Ops:
  3.6 24.4 %scatter_fusion.1 = bf16[128,2,7]{1,0,2:T(8,128)(2,1)S(1)} fusion(bf16[128,2,7]{1,0,2:T(8,128)(2,1)S(1)} %broadcast_in_dim.21, s32[512]{0:T(512)S(1)} %bitcast.45, bf16[512,2]{1,0:T(8,128)(2,1)S(1)} %broadcast_in_dim.45), kind=kCustom, calls=%fused_computation.2 | custom fusion | bytes 10240 | tf_op jit(solution)/shard_map/scatter | solution.py:28
  29.5 11.0 %all-to-all-start.2 = ((bf16[32,8,7]{2,1,0:T(8,128)(2,1)}), bf16[32,8,7]{2,1,0:T(8,128)(2,1)S(1)}, u32[]{:S(2)}, u32[]{:S(2)}) async-start(bf16[32,8,7]{2,1,0:T(8,128)(2,1)} %bitcast.6), calls=%async_computation.2 | async-start | bytes 131072 | tf_op jit(solution)/shard_map/all_to_all | solution.py:64
  43.3 8.7 %reshape.158 = bf16[512,2,1792]{2,1,0:T(2,128)(2,1)} reshape(bf16[128,4,3584]{2,1,0:T(4,128)(2,1)} %broadcast_in_dim.47) | data formatting | bytes 7340032 | tf_op jit(solution)/shard_map/reshape;reshape | solution.py:24
  56.4 69.8 %scatter_fusion.2 = bf16[128,2,7,1792]{3,1,2,0:T(2,128)(2,1)} fusion(bf16[128,2,7,1792]{3,1,2,0:T(2,128)(2,1)} %broadcast_in_dim.46, s32[512]{0:T(512)S(1)} %bitcast.46, bf16[512,2,1792]{2,1,0:T(2,128)(2,1)} %reshape.158), kind=kCustom, calls=%fused_computation.3 | custom fusion | bytes 11014144 | tf_op jit(solution)/shard_map/scatter | solution.py:23
  133.0 13.8 %reshape.133 = bf16[32,8,7,1792]{3,1,0,2:T(8,128)(2,1)} reshape(bf16[128,2,7,1792]{3,1,0,2:T(2,128)(2,1)} %copy.60) | data formatting | bytes 12845056 | tf_op jit(solution)/shard_map/reshape | solution.py:39
  152.7 9.3 %all-to-all-start.4 = ((bf16[32,8,7,1792]{3,1,2,0:T(8,128)(2,1)}), bf16[32,8,7,1792]{3,1,2,0:T(8,128)(2,1)}, u32[]{:S(2)}, u32[]{:S(2)}) async-start(bf16[32,8,7,1792]{3,1,2,0:T(8,128)(2,1)} %copy.61), calls=%async_computation.4 | async-start | bytes 12845056 | tf_op jit(solution)/shard_map/all_to_all | solution.py:38
  162.7 138.4 %all-to-all-done.4 = bf16[32,8,7,1792]{3,1,2,0:T(8,128)(2,1)} async-done(((bf16[32,8,7,1792]{3,1,2,0:T(8,128)(2,1)}), bf16[32,8,7,1792]{3,1,2,0:T(8,128)(2,1)}, u32[]{:S(2)}, u32[]{:S(2)}) %all-to-all-start.4) | async-done | bytes 6422560 | tf_op jit(solution)/shard_map/all_to_all | solution.py:38
  301.1 8.1 all-to-all-start.3
  326.8 62.7 %scatter_fusion = bf16[128,2,7,1024]{3,1,2,0:T(2,128)(2,1)} fusion(bf16[128,2,7,1024]{3,1,2,0:T(2,128)(2,1)} %broadcast_in_dim.18, s32[512]{0:T(512)S(1)} %bitcast.47, bf16[512,2,1024]{2,1,0:T(2,128)(2,1)S(1)} %broadcast_in_dim.20), kind=kCustom, calls=%fused_computation.1 | custom fusion | bytes 6295552 | tf_op jit(solution)/shard_map/scatter | solution.py:33
  406.8 9.7 %all-to-all-start = ((bf16[32,8,7,1024]{3,1,2,0:T(8,128)(2,1)}), bf16[32,8,7,1024]{3,1,2,0:T(8,128)(2,1)}, u32[]{:S(2)}, u32[]{:S(2)}) async-start(bf16[32,8,7,1024]{3,1,2,0:T(8,128)(2,1)} %copy.55), calls=%async_computation | async-start | bytes 7340032 | tf_op jit(solution)/shard_map/all_to_all | solution.py:51
  416.6 12.4 %fusion.2 = f32[32,8,7,1024]{3,0,2,1:T(8,128)} fusion(bf16[32,8,7,1792]{3,0,2,1:T(8,128)(2,1)} %all-to-all-done.5, bf16[1,1024,1792]{2,1,0:T(8,128)(2,1)} %param.9), kind=kOutput, calls=%fused_computation.8 | convolution fusion | flops 6576668672 | bytes 17432576 | tf_op jit(solution)/shard_map/dot_general | solution.py:81
  428.9 69.6 %all-to-all-done = bf16[32,8,7,1024]{3,1,2,0:T(8,128)(2,1)} async-done(((bf16[32,8,7,1024]{3,1,2,0:T(8,128)(2,1)}), bf16[32,8,7,1024]{3,1,2,0:T(8,128)(2,1)}, u32[]{:S(2)}, u32[]{:S(2)}) %all-to-all-start) | async-done | bytes 3670048 | tf_op jit(solution)/shard_map/all_to_all | solution.py:51
  498.6 7.1 all-to-all-start.6
  511.6 76.5 %all-to-all-done.6 = f32[32,8,7,1024]{3,0,2,1:T(8,128)} async-done(((f32[32,8,7,1024]{3,0,2,1:T(8,128)}), f32[32,8,7,1024]{3,0,2,1:T(8,128)}, u32[]{:S(2)}, u32[]{:S(2)}) %all-to-all-start.6) | async-done | bytes 7340064 | tf_op jit(solution)/shard_map/all_to_all | solution.py:91
  593.5 10.3 %copy.66 = f32[32,8,7,1024]{3,1,2,0:T(8,128)} copy(f32[32,8,7,1024]{3,0,2,1:T(8,128)} %all-to-all-done.6) | data formatting | bytes 14680064 | tf_op jit(solution)/shard_map/all_to_all | solution.py:91
  603.8 32.8 %all-to-all-done.1 = bf16[32,8,7,1024]{3,0,2,1:T(8,128)(2,1)} async-done(((bf16[32,8,7,1024]{3,0,2,1:T(8,128)(2,1)}), bf16[32,8,7,1024]{3,0,2,1:T(8,128)(2,1)}, u32[]{:S(2)}, u32[]{:S(2)}) %all-to-all-start.1) | async-done | bytes 3670048 | tf_op jit(solution)/shard_map/all_to_all | solution.py:50
  636.7 7.6 all-to-all-start.7
  644.4 12.4 %fusion.4 = bf16[1,1024,1792]{2,1,0:T(8,128)(2,1)} fusion(bf16[32,8,7,1024]{3,0,2,1:T(8,128)(2,1)} %all-to-all-done.1, bf16[32,8,7,1792]{3,0,2,1:T(8,128)(2,1)} %all-to-all-done.5, f32[32,8,7]{0,2,1:T(8,128)S(1)} %convert_element_type.56), kind=kOutput, calls=%fused_computation.10 | convolution fusion | flops 6588137472 | bytes 13769728 | tf_op jit(solution)/shard_map/dot_general | solution.py:87
  656.8 149.4 %all-to-all-done.7 = f32[32,8,7,1024]{3,1,2,0:T(8,128)} async-done(((f32[32,8,7,1024]{3,1,2,0:T(8,128)}), f32[32,8,7,1024]{3,1,2,0:T(8,128)}, u32[]{:S(2)}, u32[]{:S(2)}) %all-to-all-start.7) | async-done | bytes 7340064 | tf_op jit(solution)/shard_map/all_to_all | solution.py:90
  806.2 7.5 copy.67
  813.7 9.9 %reshape.134 = f32[128,2,7,1024]{3,1,0,2:T(2,128)} reshape(f32[32,8,7,1024]{3,1,0,2:T(8,128)} %copy.67) | data formatting | bytes 14680064 | tf_op jit(solution)/shard_map/reshape | solution.py:103
  823.6 8.6 copy.68
  832.2 12.6 %gather_fusion = f32[512,2,1024]{2,1,0:T(2,128)} fusion(f32[128,2,7,1024]{3,1,2,0:T(2,128)} %copy.68, s32[512]{0:T(512)S(1)} %bitcast.48), kind=kCustom, calls=%fused_computation | custom fusion | bytes 8392704 | tf_op jit(solution)/shard_map/gather | solution.py:103
  844.9 12.1 %fusion.13 = (f32[512,1024]{1,0:T(8,128)}, f32[512,1,1024]{2,1,0:T(1,128)S(1)}) fusion(f32[512,2,1024]{2,1,0:T(2,128)} %gather_fusion), kind=kLoop, calls=%fused_computation.34 | loop fusion | flops 1572864 | bytes 8388608 | tf_op jit(solution)/shard_map/convert_element_type | solution.py:105
  (51 shorter events, 75.6 us)
Async XLA Ops:
  0.6 39.9 %copy-start.1 = (bf16[128,3584]{1,0:T(8,128)(2,1)S(1)}, bf16[128,3584]{1,0:T(8,128)(2,1)}, u32[]{:S(2)}) copy-start(bf16[128,3584]{1,0:T(8,128)(2,1)} %param.5) | copy-start | bytes 2752516
  29.5 123.1 %all-to-all-start.2 = ((bf16[32,8,7]{2,1,0:T(8,128)(2,1)}), bf16[32,8,7]{2,1,0:T(8,128)(2,1)S(1)}, u32[]{:S(2)}, u32[]{:S(2)}) async-start(bf16[32,8,7]{2,1,0:T(8,128)(2,1)} %bitcast.6), calls=%async_computation.2 | async-start | bytes 131072 | tf_op jit(solution)/shard_map/all_to_all | solution.py:64
  152.7 148.5 %all-to-all-start.4 = ((bf16[32,8,7,1792]{3,1,2,0:T(8,128)(2,1)}), bf16[32,8,7,1792]{3,1,2,0:T(8,128)(2,1)}, u32[]{:S(2)}, u32[]{:S(2)}) async-start(bf16[32,8,7,1792]{3,1,2,0:T(8,128)(2,1)} %copy.61), calls=%async_computation.4 | async-start | bytes 12845056 | tf_op jit(solution)/shard_map/all_to_all | solution.py:38
  301.1 15.1 %all-to-all-start.3 = ((bf16[32,8,7]{0,2,1:T(8,128)(2,1)}), bf16[32,8,7]{0,2,1:T(8,128)(2,1)S(1)}, u32[]{:S(2)}, u32[]{:S(2)}) async-start(bf16[32,8,7]{0,2,1:T(8,128)(2,1)} %copy.59), calls=%async_computation.3 | async-start | bytes 32768 | tf_op jit(solution)/shard_map/all_to_all | solution.py:63
  316.2 5.5 copy-start
  316.2 90.6 %all-to-all-start.5 = ((bf16[32,8,7,1792]{3,0,2,1:T(8,128)(2,1)}), bf16[32,8,7,1792]{3,0,2,1:T(8,128)(2,1)}, u32[]{:S(2)}, u32[]{:S(2)}) async-start(bf16[32,8,7,1792]{3,0,2,1:T(8,128)(2,1)} %copy.62), calls=%async_computation.5 | async-start | bytes 12845056 | tf_op jit(solution)/shard_map/all_to_all | solution.py:37
  406.8 91.7 %all-to-all-start = ((bf16[32,8,7,1024]{3,1,2,0:T(8,128)(2,1)}), bf16[32,8,7,1024]{3,1,2,0:T(8,128)(2,1)}, u32[]{:S(2)}, u32[]{:S(2)}) async-start(bf16[32,8,7,1024]{3,1,2,0:T(8,128)(2,1)} %copy.55), calls=%async_computation | async-start | bytes 7340032 | tf_op jit(solution)/shard_map/all_to_all | solution.py:51
  498.6 89.6 %all-to-all-start.6 = ((f32[32,8,7,1024]{3,0,2,1:T(8,128)}), f32[32,8,7,1024]{3,0,2,1:T(8,128)}, u32[]{:S(2)}, u32[]{:S(2)}) async-start(f32[32,8,7,1024]{3,0,2,1:T(8,128)} %fusion.2), calls=%async_computation.6 | async-start | bytes 14680064 | tf_op jit(solution)/shard_map/all_to_all | solution.py:91
  588.1 48.5 %all-to-all-start.1 = ((bf16[32,8,7,1024]{3,0,2,1:T(8,128)(2,1)}), bf16[32,8,7,1024]{3,0,2,1:T(8,128)(2,1)}, u32[]{:S(2)}, u32[]{:S(2)}) async-start(bf16[32,8,7,1024]{3,0,2,1:T(8,128)(2,1)} %copy.56), calls=%async_computation.1 | async-start | bytes 7340032 | tf_op jit(solution)/shard_map/all_to_all | solution.py:50
  603.8 40.4 %copy-start.2 = (bf16[128,4]{0,1:T(4,128)(2,1)S(1)}, bf16[128,4]{0,1:T(4,128)(2,1)}, u32[]{:S(2)}) copy-start(bf16[128,4]{0,1:T(4,128)(2,1)} %param.7) | copy-start | bytes 3076
  636.7 169.5 %all-to-all-start.7 = ((f32[32,8,7,1024]{3,1,2,0:T(8,128)}), f32[32,8,7,1024]{3,1,2,0:T(8,128)}, u32[]{:S(2)}, u32[]{:S(2)}) async-start(f32[32,8,7,1024]{3,1,2,0:T(8,128)} %copy.66), calls=%async_computation.7 | async-start | bytes 14680064 | tf_op jit(solution)/shard_map/all_to_all | solution.py:90
where the time goes:
time: 875 us; the launch traced here: 862 us
  waiting for transfers between devices  467 us (53%)
  local copies, waits for them, and re-layouts  291 us (33%)
  starting transfers between devices  63.7 us (7%)
  matrix products  24.8 us (3%)
  other arithmetic  14.4 us (2%)
    all_to_all x1, waiting for transfers between devices, local(): lax.all_to_all(lax.all_to_all(partial_value.reshape(groups, members, capa...  149 us
    all_to_all x1, waiting for transfers between devices, local(): lax.all_to_all(grad_buffer.reshape(groups, members, capacity, half_width)...  138 us
    scatter x2, local copies, waits for them, and re-layouts, local(): grad_buffer.at[targets, :, positions]  76.6 us
    all_to_all x1, waiting for transfers between devices, local(): lax.all_to_all(partial_value.reshape(groups, members, capacity, hidden_un...  76.5 us
    all_to_all x1, waiting for transfers between devices, local(): lax.all_to_all(hidden_buffer.reshape(groups, members, capacity, hidden_bu...  69.6 us
    scatter x2, local copies, waits for them, and re-layouts, local(): hidden_buffer.at[targets, :, positions]  69.1 us
    all_to_all x1, waiting for transfers between devices, local(): lax.all_to_all(lax.all_to_all(hidden_buffer.reshape(groups, members, capa...  32.8 us
    scatter x2, local copies, waits for them, and re-layouts, local(): gate_buffer.at[targets, :, positions]  25.9 us
  transfers between devices with their start and end apart: 8, of which 5 were waited for; matrix products, arithmetic and copies ran while one was open for 29% of the time, Pallas kernels for 0%

commit v1 on v0

v1 whole, which is shorter than its diff:
```python
import functools

import jax
import jax.numpy as jnp
from jax import lax
from jax.experimental import pallas as pl
from jax.experimental.pallas import tpu as pltpu
from jax.sharding import PartitionSpec as P

MESH = pl.DeviceIdType.MESH
NX = 4
PAD = 8
BLK = 2 * PAD


class Place:
    def __init__(self, groups, members):
        self.nx = NX
        self.nz = groups // NX
        self.ny = members // 2
        self.plane = self.nx * self.ny
        g = lax.axis_index("group")
        m = lax.axis_index("members")
        self.x = g // self.nz
        self.z = lax.rem(g, self.nz)
        self.y = m // 2
        self.c = lax.rem(m, 2)
        self.a = self.x * self.ny + self.y

    def dev(self, x, z, y, c):
        return (x * self.nz + z, y * 2 + c)

    def sibling(self):
        return self.dev(self.x, self.z, self.y, 1 - self.c)

    def along_z(self, step):
        z = lax.rem(self.z + step + self.nz, self.nz)
        return z, self.dev(self.x, z, self.y, self.c)

    def in_plane(self, i):
        x = lax.rem(self.x + i // self.ny, self.nx)
        y = lax.rem(self.y + lax.rem(i, self.ny), self.ny)
        return x * self.ny + y, self.dev(x, self.z, y, self.c)

    def greet(self):
        barrier = pltpu.get_barrier_semaphore()
        pl.semaphore_signal(barrier, inc=1, device_id=self.sibling(), device_id_type=MESH)

        @pl.loop(1, self.nz)
        def _(j):
            pl.semaphore_signal(
                barrier, inc=1, device_id=self.along_z(j)[1], device_id_type=MESH
            )

        @pl.loop(1, self.plane)
        def _(i):
            pl.semaphore_signal(
                barrier, inc=1, device_id=self.in_plane(i)[1], device_id_type=MESH
            )

        pl.semaphore_wait(barrier, self.nz + self.plane - 1)


def remote(src, dst, ssem, rsem, device):
    return pltpu.make_async_remote_copy(
        src_ref=src, dst_ref=dst, send_sem=ssem, recv_sem=rsem, device_id=device, device_id_type=MESH
    )


def route_hits(ids, rows):
    parts = []
    for core in range(2):
        for k in range(ids.shape[1] // 2):
            hit = rows == ids[core, k : k + 1, :]
            parts.append(jnp.where(hit, 1.0, 0.0).astype(jnp.bfloat16))
    return jnp.concatenate(parts, axis=1)


def token_hits(ids, rows):
    parts = []
    for core in range(2):
        hit = rows == ids[core, 0:1, :]
        for k in range(1, ids.shape[1] // 2):
            hit = hit | (rows == ids[core, k : k + 1, :])
        parts.append(jnp.where(hit, 1.0, 0.0).astype(jnp.bfloat16))
    return jnp.concatenate(parts, axis=1)


def dispatch_kernel(
    groups, members,
    og, hs, sid,
    rb, hf, ids_out,
    gat, ids, sb, h0, hsend, hmid,
    x_s, x_r, x_l, ag_s, ag_r, agm_s, agm_r,
    p_s, p_r, p_l, hp_s, hp_r, hp_l, hz_s, hz_r, hz_l, hx_s, hx_r, out_l,
):
    me = Place(groups, members)
    nz, plane = me.nz, me.plane
    half_d = gat.shape[2]
    half_f = h0.shape[1]
    tok = og.shape[0]
    n_routes = hs.shape[0]
    z, c, a = me.z, me.c, me.a
    steps = nz // 2
    chunk = plane * BLK

    me.greet()

    def cols(n, which):
        return pl.ds(pl.multiple_of(which * n, n), n)

    own = [
        (og.at[:, cols(half_d, c)], gat.at[z, pl.ds(pl.multiple_of(c * tok, tok), tok)]),
        (hs.at[:, cols(half_f, c)], h0.at[pl.ds(pl.multiple_of(c * n_routes, n_routes), n_routes)]),
        (sid, ids.at[z, c]),
    ]
    away = [
        og.at[:, cols(half_d, 1 - c)],
        hs.at[:, cols(half_f, 1 - c)],
        sid,
    ]
    give = [
        remote(src, dst, x_s.at[i], x_r.at[i], me.sibling())
        for i, (src, (_, dst)) in enumerate(zip(away, own))
    ]
    keep = [pltpu.make_async_copy(src, dst, x_l.at[i]) for i, (src, dst) in enumerate(own)]
    for op in give:
        op.start()
    for op in keep:
        op.start()
    for op in keep:
        op.wait()
    for op in give:
        op.wait_recv()

    def ring(way, step, half):
        block = lax.rem(z - step + nz, nz) if way == 0 else lax.rem(z + step, nz)
        _, target = me.along_z(1 if way == 0 else -1)
        rows = gat.at[block, half * tok : (half + 1) * tok]
        table = ids.at[block, half]
        return (
            remote(rows, rows, ag_s.at[way, step, half], ag_r.at[way, step, half], target),
            remote(table, table, agm_s.at[way, step, half], agm_r.at[way, step, half], target),
        )

    def ring_start(way, step, half):
        for op in ring(way, step, half):
            op.start()

    def ring_arrive(way, step, half):
        for op in ring(way, step, half):
            op.wait_recv()

    for half in range(2):
        ring_start(0, 0, half)
        ring_start(1, 0, half)

    def spread(block):
        rows = lax.broadcasted_iota(jnp.int32, (chunk, 1), 0) + z * chunk
        hits = token_hits(ids[block], rows)
        width = half_d // 7 if half_d % (7 * 128) == 0 else half_d
        for t in range(half_d // width):
            picked = jnp.dot(
                hits, gat[block, :, t * width : (t + 1) * width], preferred_element_type=jnp.float32
            )
            sb[block, :, :, t * width : (t + 1) * width] = picked.astype(jnp.bfloat16).reshape(
                plane, BLK, width
            )

        @pl.loop(1, plane)
        def _(i):
            q, target = me.in_plane(i)
            remote(sb.at[block, q], rb.at[block, a], p_s.at[block], p_r.at[block], target).start()

        pltpu.make_async_copy(sb.at[block, a], rb.at[block, a], p_l.at[block]).start()

    def spread_hidden():
        per_x = me.ny * nz * BLK

        @pl.loop(0, me.nx)
        def _(dx):
            row = lax.broadcasted_iota(jnp.int32, (per_x, 1), 0)
            xq = lax.rem(me.x + dx, me.nx)
            slot = lax.rem(row, BLK)
            zq = lax.rem(row // BLK, nz)
            yq = row // (BLK * nz)
            rows = zq * chunk + (xq * me.ny + yq) * BLK + slot
            hits = route_hits(ids[z], rows)
            picked = jnp.dot(hits, h0[...], preferred_element_type=jnp.float32)
            hsend[pl.ds(xq * me.ny, me.ny)] = picked.astype(jnp.bfloat16).reshape(
                me.ny, nz, BLK, half_f
            )

        @pl.loop(1, plane)
        def _(i):
            q, target = me.in_plane(i)
            remote(hsend.at[q], hmid.at[a], hp_s.at[0], hp_r.at[0], target).start()

        pltpu.make_async_copy(hsend.at[a], hmid.at[a], hp_l.at[0]).start()

    def hidden_arrive():
        pltpu.make_async_copy(
            hmid.at[pl.ds(0, plane - 1)], hmid.at[pl.ds(0, plane - 1)], hp_r.at[0]
        ).wait()
        pltpu.make_async_copy(hsend.at[a], hmid.at[a], hp_l.at[0]).wait()

    def hidden_hop(j):
        to, target = me.along_z(j)
        return remote(hmid.at[:, to], hf.at[c, z], hz_s.at[j], hz_r.at[j], target)

    def hidden_share(j):
        frm = lax.rem(z - j + nz, nz)
        return remote(hf.at[c, frm], hf.at[c, frm], hx_s.at[j], hx_r.at[j], me.sibling())

    spread(z)
    spread_hidden()

    @pl.loop(1, nz)
    def _(o):
        step = (o - 1) // 2
        up = lax.rem(o, 2) == 1
        last = o == nz - 1

        @pl.when(last)
        def _():
            ring_arrive(0, steps - 1, 0)
            ring_arrive(1, steps - 1, 1)

        @pl.when(jnp.logical_and(up, jnp.logical_not(last)))
        def _():
            ring_arrive(0, step, 0)
            ring_arrive(0, step, 1)
            ring_start(0, step + 1, 0)

            @pl.when(step + 1 < steps - 1)
            def _():
                ring_start(0, step + 1, 1)

        @pl.when(jnp.logical_not(up))
        def _():
            ring_arrive(1, step, 0)
            ring_arrive(1, step, 1)
            ring_start(1, step + 1, 1)

            @pl.when(step + 1 < steps - 1)
            def _():
                ring_start(1, step + 1, 0)

        block = jnp.where(up, lax.rem(z - 1 - step + nz, nz), lax.rem(z + 1 + step, nz))
        spread(block)

        @pl.when(o == nz - 2)
        def _():
            hidden_arrive()
            pltpu.make_async_copy(hmid.at[:, z], hf.at[c, z], hz_l.at[0]).start()

            @pl.loop(1, nz)
            def _(j):
                hidden_hop(j).start()

    pltpu.make_async_copy(hmid.at[:, z], hf.at[c, z], hz_l.at[0]).wait()
    hidden_share(0).start()

    @pl.loop(1, nz)
    def _(j):
        hidden_hop(j).wait_recv()
        hidden_share(j).start()

    table = pltpu.make_async_copy(ids.at[z], ids_out, out_l.at[0])
    table.start()
    table.wait()

    @pl.loop(0, nz)
    def _(block):
        pltpu.make_async_copy(
            rb.at[block, pl.ds(0, plane - 1)], rb.at[block, pl.ds(0, plane - 1)], p_r.at[block]
        ).wait()
        pltpu.make_async_copy(
            sb.at[block, pl.ds(0, plane - 1)], sb.at[block, pl.ds(0, plane - 1)], p_s.at[block]
        ).wait()
        pltpu.make_async_copy(sb.at[block, a], rb.at[block, a], p_l.at[block]).wait()
        hidden_share(block).wait()

    @pl.loop(1, nz)
    def _(j):
        hidden_hop(j).wait_send()

    pltpu.make_async_copy(
        hsend.at[pl.ds(0, plane - 1)], hsend.at[pl.ds(0, plane - 1)], hp_s.at[0]
    ).wait()
    for op in give:
        op.wait_send()
    for step in range(steps):
        for way in range(2):
            for half in range(2):
                if step < steps - 1 or way == half:
                    for op in ring(way, step, half):
                        op.wait_send()


def return_kernel(
    groups, members,
    part, ids_in,
    out,
    own, got, ret, rmid, rr, acc, both, ids,
    o_l, e_s, e_r, p_s, p_r, p_l, z_s, z_r, z_l, u_s, u_r, u_l, i_l,
):
    me = Place(groups, members)
    nz, plane = me.nz, me.plane
    z, c, a = me.z, me.c, me.a
    half_f = own.shape[3]
    chunk = plane * BLK
    n_routes = both.shape[1]

    me.greet()
    table = pltpu.make_async_copy(ids_in, ids, i_l.at[0])
    table.start()

    def cols(which):
        return pl.ds(pl.multiple_of(which * half_f, half_f), half_f)

    def order(o):
        return lax.rem(z + nz // 2 + o, nz)

    def mine(o):
        b = order(o)
        return pltpu.make_async_copy(part.at[b, :, :, cols(c)], own.at[b], o_l.at[b])

    def other(o):
        b = order(o)
        return remote(part.at[b, :, :, cols(1 - c)], got.at[b], e_s.at[b], e_r.at[b], me.sibling())

    @pl.loop(0, nz)
    def _(o):
        mine(o).start()
        other(o).start()

    table.wait()

    def hop(b):
        return remote(rmid.at[b], rr.at[z], z_s.at[b], z_r.at[z], me.dev(me.x, b, me.y, c))

    @pl.loop(0, nz)
    def _(o):
        b = order(o)
        mine(o).wait()
        other(o).wait_recv()
        ret[b] = (own[b] + got[b]).astype(jnp.bfloat16)

        @pl.loop(1, plane)
        def _(i):
            q, target = me.in_plane(i)
            remote(ret.at[b, q], rmid.at[b, a], p_s.at[b], p_r.at[b], target).start()

        pltpu.make_async_copy(ret.at[b, a], rmid.at[b, a], p_l.at[b]).start()

    @pl.loop(0, nz)
    def _(o):
        b = order(o)
        pltpu.make_async_copy(
            rmid.at[b, pl.ds(0, plane - 1)], rmid.at[b, pl.ds(0, plane - 1)], p_r.at[b]
        ).wait()
        pltpu.make_async_copy(ret.at[b, a], rmid.at[b, a], p_l.at[b]).wait()

        @pl.when(b != z)
        def _():
            hop(b).start()

        @pl.when(b == z)
        def _():
            pltpu.make_async_copy(rmid.at[b], rr.at[z], z_l.at[0]).start()

    acc[...] = jnp.zeros_like(acc)

    def take(b):
        rows = lax.broadcasted_iota(jnp.int32, (chunk, 1), 0) + b * chunk
        hits = route_hits(ids[...], rows)
        acc[...] += lax.dot_general(
            hits,
            rr[b].reshape(chunk, half_f),
            (((0,), (0,)), ((), ())),
            preferred_element_type=jnp.float32,
        )

    pltpu.make_async_copy(rmid.at[z], rr.at[z], z_l.at[0]).wait()
    take(z)

    @pl.loop(1, nz)
    def _(j):
        b = lax.rem(z + j, nz)
        pltpu.make_async_copy(rr.at[b], rr.at[b], z_r.at[b]).wait()
        take(b)

    both[...] = acc[...].astype(jnp.bfloat16).reshape(both.shape)
    give = remote(both.at[1 - c], out.at[c], u_s.at[0], u_r.at[0], me.sibling())
    keep = pltpu.make_async_copy(both.at[c], out.at[c], u_l.at[0])
    give.start()
    keep.start()
    keep.wait()
    give.wait()

    @pl.loop(0, nz)
    def _(b):
        other(b).wait_send()
        pltpu.make_async_copy(
            ret.at[b, pl.ds(0, plane - 1)], ret.at[b, pl.ds(0, plane - 1)], p_s.at[b]
        ).wait()

        @pl.when(b != z)
        def _():
            hop(b).wait_send()


def dispatch(groups, members, og, hs, sid):
    nz, ny = groups // NX, members // 2
    plane = NX * ny
    tok, d = og.shape
    n_routes, f = hs.shape
    dma = pltpu.SemaphoreType.DMA
    any_ = pl.BlockSpec(memory_space=pl.ANY)
    bf = jnp.bfloat16
    steps = nz // 2
    return pl.pallas_call(
        functools.partial(dispatch_kernel, groups, members),
        name="dispatch",
        out_shape=(
            jax.ShapeDtypeStruct((nz, plane, BLK, d // 2), bf),
            jax.ShapeDtypeStruct((2, nz, plane, BLK, f // 2), bf),
            jax.ShapeDtypeStruct((2,) + sid.shape, jnp.int32),
        ),
        in_specs=[any_] * 3,
        out_specs=(any_,) * 3,
        scratch_shapes=[
            pltpu.VMEM((nz, 2 * tok, d // 2), bf),
            pltpu.VMEM((nz, 2) + sid.shape, jnp.int32),
            pltpu.VMEM((nz, plane, BLK, d // 2), bf),
            pltpu.VMEM((2 * n_routes, f // 2), bf),
            pltpu.VMEM((plane, nz, BLK, f // 2), bf),
            pltpu.VMEM((plane, nz, BLK, f // 2), bf),
            dma((3,)), dma((3,)), dma((3,)),
            dma((2, steps, 2)), dma((2, steps, 2)), dma((2, steps, 2)), dma((2, steps, 2)),
            dma((nz,)), dma((nz,)), dma((nz,)),
            dma((1,)), dma((1,)), dma((1,)),
            dma((nz,)), dma((nz,)), dma((1,)),
            dma((nz,)), dma((nz,)), dma((1,)),
        ],
        compiler_params=pltpu.CompilerParams(
            collective_id=0, has_side_effects=True, vmem_limit_bytes=60 << 20
        ),
    )(og, hs, sid)


def give_back(groups, members, part, ids):
    nz, ny = groups // NX, members // 2
    plane = NX * ny
    half_f = part.shape[3] // 2
    tok = ids.shape[2]
    n_routes = tok * (ids.shape[1] // 2)
    dma = pltpu.SemaphoreType.DMA
    any_ = pl.BlockSpec(memory_space=pl.ANY)
    bf = jnp.bfloat16
    return pl.pallas_call(
        functools.partial(return_kernel, groups, members),
        name="give_back",
        out_shape=jax.ShapeDtypeStruct((2, n_routes, half_f), bf),
        in_specs=[any_] * 2,
        out_specs=any_,
        scratch_shapes=[
            pltpu.VMEM((nz, plane, BLK, half_f), jnp.float32),
            pltpu.VMEM((nz, plane, BLK, half_f), jnp.float32),
            pltpu.VMEM((nz, plane, BLK, half_f), bf),
            pltpu.VMEM((nz, plane, BLK, half_f), bf),
            pltpu.VMEM((nz, plane, BLK, half_f), bf),
            pltpu.VMEM((2 * n_routes, half_f), jnp.float32),
            pltpu.VMEM((2, n_routes, half_f), bf),
            pltpu.VMEM(ids.shape, jnp.int32),
            dma((nz,)), dma((nz,)), dma((nz,)),
            dma((nz,)), dma((nz,)), dma((nz,)),
            dma((nz,)), dma((nz,)), dma((1,)),
            dma((1,)), dma((1,)), dma((1,)), dma((1,)),
        ],
        compiler_params=pltpu.CompilerParams(
            collective_id=1, has_side_effects=True, vmem_limit_bytes=60 << 20
        ),
    )(part, ids)


def local(out_grad, hidden_act, gate_weight, routes, down_weight):
    groups = lax.axis_size("group")
    members = lax.axis_size("members")
    nz, ny = groups // NX, members // 2
    plane = NX * ny
    tok, d = out_grad.shape
    top, f = hidden_act.shape[1:]
    rows = nz * plane * BLK
    core = lax.rem(lax.axis_index("members"), 2)

    expert = routes.T.reshape(-1)
    earlier = jnp.arange(top * tok)[None, :] < jnp.arange(top * tok)[:, None]
    same = expert[None, :] == expert[:, None]
    rank = jnp.sum((same & earlier).astype(jnp.int32), axis=1)
    ex, ez, ey = expert // (nz * ny), (expert // ny) % nz, expert % ny
    slot = (ez * plane + ex * ny + ey) * BLK + core * PAD + rank
    sid = jnp.concatenate([slot.reshape(top, tok), jnp.full((top, tok), -1, jnp.int32)], axis=0)

    gate = gate_weight.astype(jnp.float32)
    hs = (gate[:, :, None] * hidden_act.astype(jnp.float32)).astype(jnp.bfloat16)
    hs = jnp.transpose(hs, (1, 0, 2)).reshape(top * tok, f)

    rb, hf, ids = dispatch(groups, members, out_grad, hs, sid)
    grad_in = rb.reshape(rows, d // 2)
    part = lax.dot_general(
        grad_in, down_weight[0], (((1,), (1,)), ((), ())), preferred_element_type=jnp.float32
    )
    back = give_back(groups, members, part.reshape(nz, plane, BLK, f), ids)
    weight_grad = lax.dot_general(
        hf.reshape(2, rows, f // 2), grad_in, (((1,), (0,)), ((), ())),
        preferred_element_type=jnp.float32,
    ).astype(jnp.bfloat16).reshape(1, f, d // 2)

    unscaled = jnp.transpose(back.reshape(2, top, tok, f // 2), (2, 1, 0, 3)).reshape(tok, top, f)
    wide = unscaled.astype(jnp.float32)
    hidden_grad = (gate[:, :, None] * wide).astype(jnp.bfloat16)
    gate_grad = jnp.sum(wide * hidden_act.astype(jnp.float32), axis=2)
    return weight_grad, hidden_grad, gate_grad


def solution(mesh):
    both = ("group", "members")
    return jax.shard_map(
        local,
        mesh=mesh,
        in_specs=(P(both, None), P(both, None, None), P(both, None), P(both, None), P(both, None, None)),
        out_specs=(P(both, None, None), P(both, None, None), P(both, None)),
        check_vma=False,
    )
```

time: 875 us -> 248 us (0.28); the launches traced: 862 us -> 246 us
  waiting for transfers between devices: 467 us -> 0 us
  local copies, waits for them, and re-layouts: 291 us -> 9.72 us
  Pallas kernels: 0 us -> 205 us
  starting transfers between devices: 63.7 us -> 0 us
    all_to_all x8 -> x0, waiting for transfers between devices: 467 us -> none  [the longest x1 149 us: local(): lax.all_to_all(lax.all_to_all(partial_value.reshape(groups, members, capa...]
    pallas_call x0 -> x2, Pallas kernels: none -> 205 us  [the longest x1 137 us: dispatch(): pl.pallas_call(functools.partial(dispatch_kernel, groups, members), name=...]
    scatter x6 -> x0, local copies, waits for them, and re-layouts: 172 us -> none  [the longest x2 76.6 us: local(): grad_buffer.at[targets, :, positions]]
    all_to_all x8 -> x0, starting transfers between devices: 63.7 us -> none  [the longest x1 11 us: local(): lax.all_to_all(gate_buffer.reshape(groups, members, capacity), 'group', s...]
    reshape x8 -> x0, local copies, waits for them, and re-layouts: 49.4 us -> none  [the longest x2 19.7 us: local(): grad_buffer.reshape(groups, members, capacity, half_width)]
    all_to_all x5 -> x0, local copies, waits for them, and re-layouts: 31.5 us -> none  [the longest x1 10.3 us: local(): lax.all_to_all(partial_value.reshape(groups, members, capacity, hidden_un...]
    gather x1 -> x0, local copies, waits for them, and re-layouts: 12.6 us -> none  [local(): returned.reshape(experts, 2, capacity, hidden_units)[targets, :, positions]]
    broadcast_in_dim x8 -> x0, local copies, waits for them, and re-layouts: 12.5 us -> none  [the longest x1 4.38 us: local(): grad_buffer = jnp.zeros((experts, 2, capacity, half_width), jnp.bfloat16)]
  transfers between devices with their start and end apart: 8 -> 0, of which waited for: 5 -> 0; matrix products, arithmetic and copies ran while one was open for 29% -> 0% of each run, Pallas kernels for 0% -> 0%
where the time goes in v1:
time: 248 us; the launch traced here: 246 us
  Pallas kernels  205 us (83%)
  matrix products  23.6 us (10%)
  local copies, waits for them, and re-layouts  9.72 us (4%)
  other arithmetic  6.79 us (3%)
    pallas_call x1, Pallas kernels, dispatch(): pl.pallas_call(functools.partial(dispatch_kernel, groups, members), name=...  137 us
    pallas_call x1, Pallas kernels, give_back(): pl.pallas_call(functools.partial(return_kernel, groups, members), name='g...  68.2 us
    dot_general x1, matrix products, local(): lax.dot_general(hf.reshape(2, rows, f // 2), grad_in, (((1,), (0,)), ((),...  13.2 us
    dot_general x1, matrix products, local(): lax.dot_general(grad_in, down_weight[0], (((1,), (1,)), ((), ())), prefer...  10.4 us
    convert_element_type x2, local copies, waits for them, and re-layouts, local(): wide = unscaled.astype(jnp.float32)  6.38 us

profile of v1, /device:TPU:5, one launch (start us, length us, event | category | flops | bytes accessed | tf_op | source)
XLA Modules:
  0.0 245.9 jit_solution(13931765691276710614)
XLA Ops:
  0.6 1.0 convert_reduce_fusion
  1.6 0.7 fusion.16
  2.3 0.6 concatenate.3.sid
  2.9 0.8 copy.15
  3.7 1.7 fusion.8
  5.4 1.3 copy.16
  6.7 136.9 %dispatch.1 = (bf16[8,16,16,1792]{3,2,1,0:T(8,128)(2,1)}, bf16[2,8,16,16,512]{4,3,2,1,0:T(8,128)(2,1)}, s32[2,8,128]{2,1,0:T(8,128)}) custom-call(bf16[128,3584]{1,0:T(8,128)(2,1)} %og.1, bf16[512,1024]{1,0:T(8,128)(2,1)} %bitcast.50, s32[8,128]{1,0:T(8,128)} %concatenate.3.sid), custom_call_target="tpu_custom_call" | custom-call | tf_op jit(solution)/shard_map/dispatch/pallas_call | solution.py:423
  143.7 0.0 copy-start.1
  143.7 0.0 copy-start.2
  143.7 13.2 %bitcast_convert_fusion = bf16[2,512,1792]{2,1,0:T(8,128)(2,1)} fusion(bf16[2,8,16,16,512]{4,3,2,1,0:T(8,128)(2,1)} %get-tuple-element.6, bf16[8,16,16,1792]{3,2,1,0:T(8,128)(2,1)} %get-tuple-element.7), kind=kOutput, calls=%fused_computation | convolution fusion | flops 7518027776 | bytes 15204352 | tf_op jit(solution)/shard_map/dot_general | solution.py:516
  156.9 0.0 copy-done.1
  156.9 0.0 copy-done.2
  156.9 10.4 %fusion.4.part = f32[8,16,16,1024]{3,2,1,0:T(8,128)} fusion(bf16[8,16,16,1792]{3,2,1,0:T(8,128)(2,1)S(1)} %copy-done.1, bf16[1,1024,1792]{2,1,0:T(8,128)(2,1)S(1)} %copy-done.2), kind=kOutput, calls=%fused_computation.3 | convolution fusion | flops 7516192768 | bytes 19398656 | tf_op jit(solution)/shard_map/dot_general | solution.py:512
  167.3 68.2 %give_back.1 = bf16[2,512,512]{2,1,0:T(8,128)(2,1)} custom-call(f32[8,16,16,1024]{3,2,1,0:T(8,128)} %fusion.4.part, s32[2,8,128]{2,1,0:T(8,128)} %get-tuple-element.8.ids_in), custom_call_target="tpu_custom_call" | custom-call | tf_op jit(solution)/shard_map/give_back/pallas_call | solution.py:462
  235.5 1.5 convert_bitcast_fusion
  237.0 0.0 copy-start
  237.0 3.0 %copy.18 = f32[128,4,2,512]{3,2,1,0:T(2,128)} copy(f32[128,4,2,512]{3,0,1,2:T(8,128)S(1)} %convert_bitcast_fusion) | data formatting | bytes 4194304 | tf_op jit(solution)/shard_map/convert_element_type | solution.py:522
  240.0 3.4 %reshape.31 = f32[128,4,1024]{2,1,0:T(4,128)S(1)} reshape(f32[128,4,2,512]{3,2,1,0:T(2,128)} %copy.18) | data formatting | bytes 4194304 | tf_op jit(solution)/shard_map/convert_element_type | solution.py:522
  243.4 0.0 copy-done
  243.4 1.9 fusion.7
  245.3 0.7 copy.19
Async XLA Ops:
  143.7 13.2 %copy-start.1 = (bf16[8,16,16,1792]{3,2,1,0:T(8,128)(2,1)S(1)}, bf16[8,16,16,1792]{3,2,1,0:T(8,128)(2,1)}, u32[]{:S(2)}) copy-start(bf16[8,16,16,1792]{3,2,1,0:T(8,128)(2,1)} %get-tuple-element.7) | copy-start | bytes 22020100
  143.7 13.2 %copy-start.2 = (bf16[1,1024,1792]{2,1,0:T(8,128)(2,1)S(1)}, bf16[1,1024,1792]{2,1,0:T(8,128)(2,1)}, u32[]{:S(2)}) copy-start(bf16[1,1024,1792]{2,1,0:T(8,128)(2,1)} %param.9) | copy-start | bytes 11010052
  237.0 6.4 %copy-start = (bf16[128,4,1024]{2,1,0:T(4,128)(2,1)S(1)}, bf16[128,4,1024]{2,1,0:T(4,128)(2,1)}, u32[]{:S(2)}) copy-start(bf16[128,4,1024]{2,1,0:T(4,128)(2,1)} %param.6) | copy-start | bytes 3145732

commit v2 on v1

v2 whole, which is shorter than its diff:
```python
import functools

import jax
import jax.numpy as jnp
from jax import lax
from jax.experimental import pallas as pl
from jax.experimental.pallas import tpu as pltpu
from jax.sharding import PartitionSpec as P

MESH = pl.DeviceIdType.MESH
NX = 4
PAD = 8
BLK = 2 * PAD


class Place:
    def __init__(self, groups, members):
        self.nx = NX
        self.nz = groups // NX
        self.ny = members // 2
        self.plane = self.nx * self.ny
        g = lax.axis_index("group")
        m = lax.axis_index("members")
        self.x = g // self.nz
        self.z = lax.rem(g, self.nz)
        self.y = m // 2
        self.c = lax.rem(m, 2)
        self.a = self.x * self.ny + self.y

    def dev(self, x, z, y, c):
        return (x * self.nz + z, y * 2 + c)

    def sibling(self):
        return self.dev(self.x, self.z, self.y, 1 - self.c)

    def along_z(self, step):
        z = lax.rem(self.z + step + self.nz, self.nz)
        return z, self.dev(self.x, z, self.y, self.c)

    def in_plane(self, i):
        x = lax.rem(self.x + i // self.ny, self.nx)
        y = lax.rem(self.y + lax.rem(i, self.ny), self.ny)
        return x * self.ny + y, self.dev(x, self.z, y, self.c)

    def greet(self):
        barrier = pltpu.get_barrier_semaphore()
        pl.semaphore_signal(barrier, inc=1, device_id=self.sibling(), device_id_type=MESH)

        @pl.loop(1, self.nz)
        def _(j):
            pl.semaphore_signal(
                barrier, inc=1, device_id=self.along_z(j)[1], device_id_type=MESH
            )

        @pl.loop(1, self.plane)
        def _(i):
            pl.semaphore_signal(
                barrier, inc=1, device_id=self.in_plane(i)[1], device_id_type=MESH
            )

        pl.semaphore_wait(barrier, self.nz + self.plane - 1)


def remote(src, dst, ssem, rsem, device):
    return pltpu.make_async_remote_copy(
        src_ref=src, dst_ref=dst, send_sem=ssem, recv_sem=rsem, device_id=device, device_id_type=MESH
    )


def route_hits(ids, rows):
    parts = []
    for core in range(2):
        for k in range(ids.shape[1] // 2):
            hit = rows == ids[core, k : k + 1, :]
            parts.append(jnp.where(hit, 1.0, 0.0).astype(jnp.bfloat16))
    return jnp.concatenate(parts, axis=1)


def token_hits(ids, rows):
    parts = []
    for core in range(2):
        hit = rows == ids[core, 0:1, :]
        for k in range(1, ids.shape[1] // 2):
            hit = hit | (rows == ids[core, k : k + 1, :])
        parts.append(jnp.where(hit, 1.0, 0.0).astype(jnp.bfloat16))
    return jnp.concatenate(parts, axis=1)


def kernel(
    groups, members,
    og, hs, sid, w_in,
    wg, out,
    gat, ids, sb, rb, w, h0, hsend, hmid, hf, lt, part, got, ret, rmid, rr, acc, both,
    x_s, x_r, x_l, ag_s, ag_r, agm_s, agm_r,
    p_s, p_r, p_l, hp_s, hp_r, hp_l, hz_s, hz_r, hz_l, hx_s, hx_r,
    e_s, e_r, r_s, r_r, r_l, z_s, z_r, z_l, u_s, u_r, u_l, w_l, wg_l,
):
    me = Place(groups, members)
    nz, plane = me.nz, me.plane
    half_d = gat.shape[2]
    half_f = h0.shape[1]
    tok = og.shape[0]
    n_routes = hs.shape[0]
    z, c, a = me.z, me.c, me.a
    steps = nz // 2
    chunk = plane * BLK
    f32, bf = jnp.float32, jnp.bfloat16
    w_tiles, w_rows = w.shape[0], w.shape[1]

    me.greet()

    def cols(n, which):
        return pl.ds(pl.multiple_of(which * n, n), n)

    def block_of(o):
        down = lax.rem(o, 2) == 0
        step = lax.div(o + 1, 2)
        return lax.rem(jnp.where(down, z + step, z - step + nz), nz)

    own = [
        (og.at[:, cols(half_d, c)], gat.at[z, pl.ds(pl.multiple_of(c * tok, tok), tok)]),
        (sid, ids.at[z, c]),
        (hs.at[:, cols(half_f, c)], h0.at[pl.ds(pl.multiple_of(c * n_routes, n_routes), n_routes)]),
    ]
    away = [og.at[:, cols(half_d, 1 - c)], sid, hs.at[:, cols(half_f, 1 - c)]]
    give = [
        remote(src, dst, x_s.at[i], x_r.at[i], me.sibling())
        for i, (src, (_, dst)) in enumerate(zip(away, own))
    ]
    keep = [pltpu.make_async_copy(src, dst, x_l.at[i]) for i, (src, dst) in enumerate(own)]
    for op in give:
        op.start()
    for op in keep:
        op.start()
    weights = pltpu.make_async_copy(w_in, w, w_l.at[0])
    weights.start()

    def ring(way, step, half):
        block = lax.rem(z - step + nz, nz) if way == 0 else lax.rem(z + step, nz)
        _, target = me.along_z(1 if way == 0 else -1)
        rows = gat.at[block, pl.ds(pl.multiple_of(half * tok, tok), tok)]
        table = ids.at[block, half]
        return (
            remote(rows, rows, ag_s.at[way, step, half], ag_r.at[way, step, half], target),
            remote(table, table, agm_s.at[way, step, half], agm_r.at[way, step, half], target),
        )

    def ring_start(way, step, half):
        for op in ring(way, step, half):
            op.start()

    def ring_arrive(way, step, half):
        for op in ring(way, step, half):
            op.wait_recv()

    keep[0].wait()
    keep[1].wait()
    ring_start(0, 0, c)
    ring_start(1, 0, c)
    give[0].wait_recv()
    give[1].wait_recv()
    ring_start(0, 0, 1 - c)
    ring_start(1, 0, 1 - c)

    def spread(block):
        rows = lax.broadcasted_iota(jnp.int32, (chunk, 1), 0) + z * chunk
        hits = token_hits(ids[block], rows)
        width = half_d // 7 if half_d % (7 * 128) == 0 else half_d
        for t in range(half_d // width):
            picked = jnp.dot(
                hits, gat[block, :, t * width : (t + 1) * width], preferred_element_type=f32
            )
            sb[block, :, :, t * width : (t + 1) * width] = picked.astype(bf).reshape(
                plane, BLK, width
            )

        @pl.loop(1, plane)
        def _(i):
            q, target = me.in_plane(i)
            remote(sb.at[block, q], rb.at[block, a], p_s.at[block], p_r.at[block], target).start()

        pltpu.make_async_copy(sb.at[block, a], rb.at[block, a], p_l.at[block]).start()

    def spread_hidden():
        per_x = me.ny * nz * BLK

        @pl.loop(0, me.nx)
        def _(dx):
            row = lax.broadcasted_iota(jnp.int32, (per_x, 1), 0)
            xq = lax.rem(me.x + dx, me.nx)
            slot = lax.rem(row, BLK)
            zq = lax.rem(row // BLK, nz)
            yq = row // (BLK * nz)
            rows = zq * chunk + (xq * me.ny + yq) * BLK + slot
            hits = route_hits(ids[z], rows)
            picked = jnp.dot(hits, h0[...], preferred_element_type=f32)
            hsend[pl.ds(xq * me.ny, me.ny)] = picked.astype(bf).reshape(me.ny, nz, BLK, half_f)

        @pl.loop(1, plane)
        def _(i):
            q, target = me.in_plane(i)
            remote(hsend.at[q], hmid.at[a], hp_s.at[0], hp_r.at[0], target).start()

        pltpu.make_async_copy(hsend.at[a], hmid.at[a], hp_l.at[0]).start()

    def hidden_arrive():
        pltpu.make_async_copy(
            hmid.at[pl.ds(0, plane - 1)], hmid.at[pl.ds(0, plane - 1)], hp_r.at[0]
        ).wait()
        pltpu.make_async_copy(hsend.at[a], hmid.at[a], hp_l.at[0]).wait()

    def hidden_hop(j):
        to, target = me.along_z(j)
        return remote(hmid.at[:, to], hf.at[c, z], hz_s.at[j], hz_r.at[j], target)

    def hidden_share(j):
        frm = lax.rem(z - j + nz, nz)
        return remote(hf.at[c, frm], hf.at[c, frm], hx_s.at[j], hx_r.at[j], me.sibling())

    def swap(b):
        return remote(
            part.at[b, 1 - c], got.at[b], e_s.at[b], e_r.at[b], me.sibling()
        )

    def multiply(o):
        b = block_of(o)
        pltpu.make_async_copy(
            rb.at[b, pl.ds(0, plane - 1)], rb.at[b, pl.ds(0, plane - 1)], p_r.at[b]
        ).wait()
        pltpu.make_async_copy(sb.at[b, a], rb.at[b, a], p_l.at[b]).wait()
        for t in range(w_tiles):
            at = t * w_rows
            part[b, at // half_f, :, at % half_f : at % half_f + w_rows] = lax.dot_general(
                rb[b].reshape(chunk, half_d),
                w[t],
                (((1,), (1,)), ((), ())),
                preferred_element_type=f32,
            )
        swap(b).start()

    def combine(o):
        b = block_of(o)
        swap(b).wait_recv()
        ret[b] = (part[b, c] + got[b]).astype(bf).reshape(plane, BLK, half_f)

        @pl.loop(1, plane)
        def _(i):
            q, target = me.in_plane(i)
            remote(ret.at[b, q], rmid.at[b, a], r_s.at[b], r_r.at[b], target).start()

        pltpu.make_async_copy(ret.at[b, a], rmid.at[b, a], r_l.at[b]).start()

    def hop(b):
        return remote(rmid.at[b], rr.at[z], z_s.at[b], z_r.at[z], me.dev(me.x, b, me.y, c))

    def pass_on(o):
        b = block_of(o)
        pltpu.make_async_copy(
            rmid.at[b, pl.ds(0, plane - 1)], rmid.at[b, pl.ds(0, plane - 1)], r_r.at[b]
        ).wait()
        pltpu.make_async_copy(ret.at[b, a], rmid.at[b, a], r_l.at[b]).wait()

        @pl.when(b != z)
        def _():
            hop(b).start()

        @pl.when(b == z)
        def _():
            pltpu.make_async_copy(rmid.at[b], rr.at[z], z_l.at[0]).start()

    spread(z)
    keep[2].wait()
    give[2].wait_recv()
    spread_hidden()
    weights.wait()

    @pl.loop(0, 2 * (steps - 1))
    def _(n):
        step = n // 2
        half = lax.rem(n, 2)
        lo = jnp.maximum(2 * step - 3, 0)
        hi = jnp.maximum(2 * step - 1, 0)
        ring_arrive(0, step, half)

        @pl.when(jnp.logical_or(step + 1 < steps - 1, half == 0))
        def _():
            ring_start(0, step + 1, half)

        ring_arrive(1, step, half)

        @pl.when(jnp.logical_or(step + 1 < steps - 1, half == 1))
        def _():
            ring_start(1, step + 1, half)

        @pl.when(half == 1)
        def _():
            @pl.loop(2 * step + 1, 2 * step + 3)
            def _(o):
                spread(block_of(o))

            @pl.loop(lo, hi)
            def _(o):
                combine(o)

        @pl.when(half == 0)
        def _():
            @pl.loop(lo, hi)
            def _(o):
                multiply(o)

    hidden_arrive()
    pltpu.make_async_copy(hmid.at[:, z], hf.at[c, z], hz_l.at[0]).start()

    @pl.loop(1, nz)
    def _(j):
        hidden_hop(j).start()

    ring_arrive(0, steps - 1, 0)
    ring_arrive(1, steps - 1, 1)
    spread(block_of(nz - 1))
    first = max(2 * steps - 5, 0)

    @pl.loop(first, nz + 3)
    def _(i):
        @pl.when(i < nz)
        def _():
            multiply(i)

        @pl.when(jnp.logical_and(i > first, i < nz + 1))
        def _():
            combine(i - 1)

        @pl.when(i >= 3)
        def _():
            pass_on(i - 3)

    pltpu.make_async_copy(hmid.at[:, z], hf.at[c, z], hz_l.at[0]).wait()
    hidden_share(0).start()

    @pl.loop(1, nz)
    def _(j):
        hidden_hop(j).wait_recv()
        hidden_share(j).start()

    for step in range(steps):
        for way in range(2):
            for half in range(2):
                if step < steps - 1 or way == half:
                    for op in ring(way, step, half):
                        op.wait_send()

    @pl.loop(0, nz)
    def _(j):
        hidden_share(j).wait()

    f_rows = lt.shape[0]
    per_half = half_f // f_rows
    d_cols = 256

    @pl.loop(0, 2 * per_half)
    def _(i):
        h = i // per_half
        at = pl.multiple_of(lax.rem(i, per_half) * f_rows, f_rows)
        lt[...] = jnp.transpose(hf[h, :, :, :, pl.ds(at, f_rows)].reshape(nz * chunk, f_rows))

        @pl.loop(0, half_d // d_cols)
        def _(t):
            span = pl.ds(pl.multiple_of(t * d_cols, d_cols), d_cols)
            tile = jnp.dot(
                lt[...], rb[:, :, :, span].reshape(nz * chunk, d_cols), preferred_element_type=f32
            )
            gat[i, pl.ds(0, f_rows), span] = tile.astype(bf)

        pltpu.make_async_copy(
            gat.at[i, pl.ds(0, f_rows)], wg.at[pl.ds(i * f_rows, f_rows)], wg_l.at[i]
        ).start()

    acc[...] = jnp.zeros_like(acc)
    pltpu.make_async_copy(rmid.at[z], rr.at[z], z_l.at[0]).wait()

    @pl.loop(0, nz)
    def _(o):
        b = block_of(o)

        @pl.when(o > 0)
        def _():
            pltpu.make_async_copy(rr.at[b], rr.at[b], z_r.at[b]).wait()

        rows = lax.broadcasted_iota(jnp.int32, (chunk, 1), 0) + b * chunk
        hits = route_hits(ids[z], rows)
        acc[...] += lax.dot_general(
            hits,
            rr[b].reshape(chunk, half_f),
            (((0,), (0,)), ((), ())),
            preferred_element_type=f32,
        )

    both[...] = acc[...].astype(bf).reshape(both.shape)
    last = remote(both.at[1 - c], out.at[c], u_s.at[0], u_r.at[0], me.sibling())
    mine = pltpu.make_async_copy(both.at[c], out.at[c], u_l.at[0])
    last.start()
    mine.start()

    @pl.loop(0, nz)
    def _(b):
        for buf, sem in ((sb, p_s), (ret, r_s)):
            pltpu.make_async_copy(
                buf.at[b, pl.ds(0, plane - 1)], buf.at[b, pl.ds(0, plane - 1)], sem.at[b]
            ).wait()
        swap(b).wait_send()

        @pl.when(b != z)
        def _():
            hop(b).wait_send()

    @pl.loop(1, nz)
    def _(j):
        hidden_hop(j).wait_send()

    pltpu.make_async_copy(
        hsend.at[pl.ds(0, plane - 1)], hsend.at[pl.ds(0, plane - 1)], hp_s.at[0]
    ).wait()
    for op in give:
        op.wait_send()

    @pl.loop(0, 2 * per_half)
    def _(i):
        pltpu.make_async_copy(
            gat.at[i, pl.ds(0, f_rows)], wg.at[pl.ds(i * f_rows, f_rows)], wg_l.at[i]
        ).wait()

    mine.wait()
    last.wait()


def exchange(groups, members, og, hs, sid, weight):
    nz, ny = groups // NX, members // 2
    plane = NX * ny
    tok, d = og.shape
    n_routes, f = hs.shape
    half_d, half_f = d // 2, f // 2
    chunk = plane * BLK
    dma = pltpu.SemaphoreType.DMA
    any_ = pl.BlockSpec(memory_space=pl.ANY)
    bf, f32 = jnp.bfloat16, jnp.float32
    steps = nz // 2
    w_rows = min(256, half_f)
    f_rows = min(256, half_f)
    vm = pltpu.VMEM
    return pl.pallas_call(
        functools.partial(kernel, groups, members),
        name="exchange",
        out_shape=(
            jax.ShapeDtypeStruct((f, half_d), bf),
            jax.ShapeDtypeStruct((2, n_routes, half_f), bf),
        ),
        in_specs=[any_] * 4,
        out_specs=(any_,) * 2,
        scratch_shapes=[
            vm((nz, 2 * tok, half_d), bf),
            vm((nz, 2) + sid.shape, jnp.int32),
            vm((nz, plane, BLK, half_d), bf),
            vm((nz, plane, BLK, half_d), bf),
            vm((f // w_rows, w_rows, half_d), bf),
            vm((2 * n_routes, half_f), bf),
            vm((plane, nz, BLK, half_f), bf),
            vm((plane, nz, BLK, half_f), bf),
            vm((2, nz, plane, BLK, half_f), bf),
            vm((f_rows, nz * chunk), bf),
            vm((nz, 2, chunk, half_f), f32),
            vm((nz, chunk, half_f), f32),
            vm((nz, plane, BLK, half_f), bf),
            vm((nz, plane, BLK, half_f), bf),
            vm((nz, plane, BLK, half_f), bf),
            vm((2 * n_routes, half_f), f32),
            vm((2, n_routes, half_f), bf),
            dma((3,)), dma((3,)), dma((3,)),
            dma((2, steps, 2)), dma((2, steps, 2)), dma((2, steps, 2)), dma((2, steps, 2)),
            dma((nz,)), dma((nz,)), dma((nz,)),
            dma((1,)), dma((1,)), dma((1,)),
            dma((nz,)), dma((nz,)), dma((1,)),
            dma((nz,)), dma((nz,)),
            dma((nz,)), dma((nz,)),
            dma((nz,)), dma((nz,)), dma((nz,)),
            dma((nz,)), dma((nz,)), dma((1,)),
            dma((1,)), dma((1,)), dma((1,)), dma((1,)), dma((f // f_rows,)),
        ],
        compiler_params=pltpu.CompilerParams(
            collective_id=0, has_side_effects=True, vmem_limit_bytes=67043328
        ),
    )(og, hs, sid, weight)


def local(out_grad, hidden_act, gate_weight, routes, down_weight):
    groups = lax.axis_size("group")
    members = lax.axis_size("members")
    nz, ny = groups // NX, members // 2
    plane = NX * ny
    tok, d = out_grad.shape
    top, f = hidden_act.shape[1:]
    core = lax.rem(lax.axis_index("members"), 2)

    expert = routes.T.reshape(-1)
    earlier = jnp.arange(top * tok)[None, :] < jnp.arange(top * tok)[:, None]
    same = expert[None, :] == expert[:, None]
    rank = jnp.sum((same & earlier).astype(jnp.int32), axis=1)
    ex, ez, ey = expert // (nz * ny), (expert // ny) % nz, expert % ny
    slot = (ez * plane + ex * ny + ey) * BLK + core * PAD + rank
    sid = jnp.concatenate([slot.reshape(top, tok), jnp.full((top, tok), -1, jnp.int32)], axis=0)

    gate = gate_weight.astype(jnp.float32)
    hs = (gate[:, :, None] * hidden_act.astype(jnp.float32)).astype(jnp.bfloat16)
    hs = jnp.transpose(hs, (1, 0, 2)).reshape(top * tok, f)

    tiles = f // min(256, f // 2)
    weight = down_weight[0].reshape(tiles, f // tiles, d // 2)
    weight_grad, back = exchange(groups, members, out_grad, hs, sid, weight)
    weight_grad = weight_grad.reshape(1, f, d // 2)

    unscaled = jnp.transpose(back.reshape(2, top, tok, f // 2), (2, 1, 0, 3)).reshape(tok, top, f)
    wide = unscaled.astype(jnp.float32)
    hidden_grad = (gate[:, :, None] * wide).astype(jnp.bfloat16)
    gate_grad = jnp.sum(wide * hidden_act.astype(jnp.float32), axis=2)
    return weight_grad, hidden_grad, gate_grad


def solution(mesh):
    both = ("group", "members")
    return jax.shard_map(
        local,
        mesh=mesh,
        in_specs=(P(both, None), P(both, None, None), P(both, None), P(both, None), P(both, None, None)),
        out_specs=(P(both, None, None), P(both, None, None), P(both, None)),
        check_vma=False,
    )
```

time: 248 us -> 218 us (0.88)
  matrix products: 23.6 us -> 0 us
  Pallas kernels: 205 us -> 192 us
  local copies, waits for them, and re-layouts: 9.72 us -> 13.9 us
    dot_general x2 -> x0, matrix products: 23.6 us -> none  [the longest x1 13.2 us: local(): lax.dot_general(hf.reshape(2, rows, f // 2), grad_in, (((1,), (0,)), ((),...]
    pallas_call x2 -> x1, Pallas kernels: 205 us -> 192 us  [exchange(): pl.pallas_call(functools.partial(kernel, groups, members), name='exchange...]
    unnamed x7 -> x8, local copies, waits for them, and re-layouts: 0.67 us -> 4.77 us
where the time goes in v2:
time: 218 us; the launch traced here: 214 us
  Pallas kernels  192 us (88%)
  local copies, waits for them, and re-layouts  13.9 us (6%)
  other arithmetic  6.82 us (3%)
    pallas_call x1, Pallas kernels, exchange(): pl.pallas_call(functools.partial(kernel, groups, members), name='exchange...  192 us
    convert_element_type x2, local copies, waits for them, and re-layouts, local(): wide = unscaled.astype(jnp.float32)  6.44 us
    unnamed x8, local copies, waits for them, and re-layouts  4.77 us

profile of v2, /device:TPU:5, one launch (start us, length us, event | category | flops | bytes accessed | tf_op | source)
XLA Modules:
  0.0 213.8 jit_solution(13998438414160042677)
XLA Ops:
  0.6 1.0 convert_reduce_fusion
  1.6 0.7 fusion.10
  2.3 0.6 concatenate.3.sid
  2.9 0.8 copy.15
  3.7 0.0 copy-start.1
  3.7 1.7 fusion.2
  5.5 1.3 copy.16
  6.8 0.0 copy-done.1
  6.8 192.4 %exchange.1 = (bf16[1024,1792]{1,0:T(8,128)(2,1)}, bf16[2,512,512]{2,1,0:T(8,128)(2,1)}) custom-call(bf16[128,3584]{1,0:T(8,128)(2,1)} %og.1, bf16[512,1024]{1,0:T(8,128)(2,1)} %bitcast.27, s32[8,128]{1,0:T(8,128)} %concatenate.3.sid, bf16[4,256,1792]{2,1,0:T(8,128)(2,1)} %bitcast.28), custom_call_target="tpu_custom_call" | custom-call | tf_op jit(solution)/shard_map/exchange/pallas_call | solution.py:450
  199.2 1.5 convert_bitcast_fusion
  200.7 2.9 %copy.17 = f32[128,4,2,512]{3,2,1,0:T(2,128)} copy(f32[128,4,2,512]{3,0,1,2:T(8,128)S(1)} %convert_bitcast_fusion) | data formatting | bytes 4194304 | tf_op jit(solution)/shard_map/convert_element_type | solution.py:521
  203.6 0.0 copy-start
  203.6 0.0 copy-start.2
  203.6 3.5 %reshape.26 = f32[128,4,1024]{2,1,0:T(4,128)S(1)} reshape(f32[128,4,2,512]{3,2,1,0:T(2,128)} %copy.17) | data formatting | bytes 4194304 | tf_op jit(solution)/shard_map/convert_element_type | solution.py:521
  207.2 0.0 copy-done
  207.2 0.0 copy-done.2
  207.2 1.9 fusion.1
  209.1 0.7 copy.18
  209.7 4.1 %copy.20 = bf16[1,1024,1792]{2,1,0:T(8,128)(2,1)} copy(bf16[1,1024,1792]{2,1,0:T(8,128)(2,1)} %bitcast.29) | data formatting | bytes 7340032
Async XLA Ops:
  3.7 3.0 %copy-start.1 = (f32[128,4]{1,0:T(8,128)}, f32[128,4]{1,0:T(8,128)S(1)}, u32[]{:S(2)}) copy-start(f32[128,4]{1,0:T(8,128)S(1)} %copy.15) | copy-start | bytes 6148
  203.6 3.5 %copy-start = (bf16[128,4,1024]{2,1,0:T(4,128)(2,1)S(1)}, bf16[128,4,1024]{2,1,0:T(4,128)(2,1)}, u32[]{:S(2)}) copy-start(bf16[128,4,1024]{2,1,0:T(4,128)(2,1)} %param.6) | copy-start | bytes 3145732
  203.6 3.5 %copy-start.2 = (f32[128,4]{1,0:T(8,128)S(1)}, f32[128,4]{1,0:T(8,128)}, u32[]{:S(2)}) copy-start(f32[128,4]{1,0:T(8,128)} %copy-done.1) | copy-start | bytes 6148

commit v3 on v2

--- a/solution.py
+++ b/solution.py
@@ -9,8 +9,9 @@
 
 MESH = pl.DeviceIdType.MESH
 NX = 4
-PAD = 8
-BLK = 2 * PAD
+BLK = 16
+CAP = 7
+SPANS = ((0, 8), (8, 4), (12, 2))
 
 
 class Place:
@@ -67,6 +68,28 @@
     )
 
 
+def used(ref, span):
+    at, n = SPANS[span]
+    return ref.at[(slice(None),) * (len(ref.shape) - 2) + (slice(at, at + n),)]
+
+
+def send_used(src, dst, ssem, rsem, device):
+    for i in range(len(SPANS)):
+        remote(used(src, i), used(dst, i), ssem.at[i], rsem.at[i], device).start()
+
+
+def wait_used(blocks, sem):
+    for i in range(len(SPANS)):
+        pltpu.make_async_copy(used(blocks, i), used(blocks, i), sem.at[i]).wait()
+
+
+def clear_rest(ref):
+    rest = (slice(None),) * (len(ref.shape) - 2) + (slice(2 * CAP, BLK),)
+    for i in range(ref.shape[0]):
+        part = ref.at[i]
+        part[rest[1:]] = jnp.zeros(part.shape[:-2] + (BLK - 2 * CAP, part.shape[-1]), ref.dtype)
+
+
 def route_hits(ids, rows):
     parts = []
     for core in range(2):
@@ -86,11 +109,18 @@
     return jnp.concatenate(parts, axis=1)
 
 
+def packed_slots(plane, shape, axis):
+    i = lax.broadcasted_iota(jnp.int32, shape, axis)
+    q = lax.shift_right_logical(i * 4682, 16)
+    w = i - q * (2 * CAP)
+    return q * BLK + w
+
+
 def kernel(
     groups, members,
     og, hs, sid, w_in,
     wg, out,
-    gat, ids, sb, rb, w, h0, hsend, hmid, hf, lt, part, got, ret, rmid, rr, acc, both,
+    gat, ids, sb, rb, w, h0, hsend, hmid, hpk, hf, lt, part, got, ret, rmid, rpk, rr, acc, both,
     x_s, x_r, x_l, ag_s, ag_r, agm_s, agm_r,
     p_s, p_r, p_l, hp_s, hp_r, hp_l, hz_s, hz_r, hz_l, hx_s, hx_r,
     e_s, e_r, r_s, r_r, r_l, z_s, z_r, z_l, u_s, u_r, u_l, w_l, wg_l,
@@ -104,6 +134,7 @@
     z, c, a = me.z, me.c, me.a
     steps = nz // 2
     chunk = plane * BLK
+    few = plane * 2 * CAP
     f32, bf = jnp.float32, jnp.bfloat16
     w_tiles, w_rows = w.shape[0], w.shape[1]
 
@@ -132,6 +163,8 @@
         op.start()
     for op in keep:
         op.start()
+    for buf in (rb, hmid, rmid):
+        clear_rest(buf)
     weights = pltpu.make_async_copy(w_in, w, w_l.at[0])
     weights.start()
 
@@ -177,7 +210,7 @@
         @pl.loop(1, plane)
         def _(i):
             q, target = me.in_plane(i)
-            remote(sb.at[block, q], rb.at[block, a], p_s.at[block], p_r.at[block], target).start()
+            send_used(sb.at[block, q], rb.at[block, a], p_s.at[block], p_r.at[block], target)
 
         pltpu.make_async_copy(sb.at[block, a], rb.at[block, a], p_l.at[block]).start()
 
@@ -199,19 +232,25 @@
         @pl.loop(1, plane)
         def _(i):
             q, target = me.in_plane(i)
-            remote(hsend.at[q], hmid.at[a], hp_s.at[0], hp_r.at[0], target).start()
+            send_used(hsend.at[q], hmid.at[a], hp_s.at[0], hp_r.at[0], target)
 
         pltpu.make_async_copy(hsend.at[a], hmid.at[a], hp_l.at[0]).start()
 
     def hidden_arrive():
-        pltpu.make_async_copy(
-            hmid.at[pl.ds(0, plane - 1)], hmid.at[pl.ds(0, plane - 1)], hp_r.at[0]
-        ).wait()
+        wait_used(hmid.at[pl.ds(0, plane - 1)], hp_r.at[0])
         pltpu.make_async_copy(hsend.at[a], hmid.at[a], hp_l.at[0]).wait()
+
+    def packing():
+        slots = packed_slots(plane, (few, 1), 0)
+        hit = slots == lax.broadcasted_iota(jnp.int32, (few, chunk), 1)
+        return jnp.where(hit, 1.0, 0.0).astype(bf)
+
+    def packed(rows):
+        return jnp.dot(packing(), rows, preferred_element_type=f32).astype(bf)
 
     def hidden_hop(j):
         to, target = me.along_z(j)
-        return remote(hmid.at[:, to], hf.at[c, z], hz_s.at[j], hz_r.at[j], target)
+        return remote(hpk.at[to], hf.at[c, z], hz_s.at[j], hz_r.at[j], target)
 
     def hidden_share(j):
         frm = lax.rem(z - j + nz, nz)
@@ -224,9 +263,7 @@
 
     def multiply(o):
         b = block_of(o)
-        pltpu.make_async_copy(
-            rb.at[b, pl.ds(0, plane - 1)], rb.at[b, pl.ds(0, plane - 1)], p_r.at[b]
-        ).wait()
+        wait_used(rb.at[b, pl.ds(0, plane - 1)], p_r.at[b])
         pltpu.make_async_copy(sb.at[b, a], rb.at[b, a], p_l.at[b]).wait()
         for t in range(w_tiles):
             at = t * w_rows
@@ -246,19 +283,18 @@
         @pl.loop(1, plane)
         def _(i):
             q, target = me.in_plane(i)
-            remote(ret.at[b, q], rmid.at[b, a], r_s.at[b], r_r.at[b], target).start()
+            send_used(ret.at[b, q], rmid.at[b, a], r_s.at[b], r_r.at[b], target)
 
         pltpu.make_async_copy(ret.at[b, a], rmid.at[b, a], r_l.at[b]).start()
 
     def hop(b):
-        return remote(rmid.at[b], rr.at[z], z_s.at[b], z_r.at[z], me.dev(me.x, b, me.y, c))
+        return remote(rpk.at[b], rr.at[z], z_s.at[b], z_r.at[z], me.dev(me.x, b, me.y, c))
 
     def pass_on(o):
         b = block_of(o)
-        pltpu.make_async_copy(
-            rmid.at[b, pl.ds(0, plane - 1)], rmid.at[b, pl.ds(0, plane - 1)], r_r.at[b]
-        ).wait()
+        wait_used(rmid.at[b, pl.ds(0, plane - 1)], r_r.at[b])
         pltpu.make_async_copy(ret.at[b, a], rmid.at[b, a], r_l.at[b]).wait()
+        rpk[b] = packed(rmid[b].reshape(chunk, half_f))
 
         @pl.when(b != z)
         def _():
@@ -266,7 +302,7 @@
 
         @pl.when(b == z)
         def _():
-            pltpu.make_async_copy(rmid.at[b], rr.at[z], z_l.at[0]).start()
+            pltpu.make_async_copy(rpk.at[b], rr.at[z], z_l.at[0]).start()
 
     spread(z)
     keep[2].wait()
@@ -309,11 +345,15 @@
                 multiply(o)
 
     hidden_arrive()
-    pltpu.make_async_copy(hmid.at[:, z], hf.at[c, z], hz_l.at[0]).start()
 
     @pl.loop(1, nz)
     def _(j):
+        to, _ = me.along_z(j)
+        hpk[to] = packed(hmid[:, to].reshape(chunk, half_f))
         hidden_hop(j).start()
+
+    hpk[z] = packed(hmid[:, z].reshape(chunk, half_f))
+    pltpu.make_async_copy(hpk.at[z], hf.at[c, z], hz_l.at[0]).start()
 
     ring_arrive(0, steps - 1, 0)
     ring_arrive(1, steps - 1, 1)
@@ -334,7 +374,7 @@
         def _():
             pass_on(i - 3)
 
-    pltpu.make_async_copy(hmid.at[:, z], hf.at[c, z], hz_l.at[0]).wait()
+    pltpu.make_async_copy(hpk.at[z], hf.at[c, z], hz_l.at[0]).wait()
     hidden_share(0).start()
 
     @pl.loop(1, nz)
@@ -361,7 +401,13 @@
     def _(i):
         h = i // per_half
         at = pl.multiple_of(lax.rem(i, per_half) * f_rows, f_rows)
-        lt[...] = jnp.transpose(hf[h, :, :, :, pl.ds(at, f_rows)].reshape(nz * chunk, f_rows))
+        for b in range(nz):
+            lt[:, b * chunk : (b + 1) * chunk] = lax.dot_general(
+                hf[h, b, :, pl.ds(at, f_rows)],
+                packing(),
+                (((0,), (0,)), ((), ())),
+                preferred_element_type=f32,
+            ).astype(bf)
 
         @pl.loop(0, half_d // d_cols)
         def _(t):
@@ -376,7 +422,7 @@
         ).start()
 
     acc[...] = jnp.zeros_like(acc)
-    pltpu.make_async_copy(rmid.at[z], rr.at[z], z_l.at[0]).wait()
+    pltpu.make_async_copy(rpk.at[z], rr.at[z], z_l.at[0]).wait()
 
     @pl.loop(0, nz)
     def _(o):
@@ -386,27 +432,26 @@
         def _():
             pltpu.make_async_copy(rr.at[b], rr.at[b], z_r.at[b]).wait()
 
-        rows = lax.broadcasted_iota(jnp.int32, (chunk, 1), 0) + b * chunk
+        rows = packed_slots(plane, (few, 1), 0) + b * chunk
         hits = route_hits(ids[z], rows)
         acc[...] += lax.dot_general(
             hits,
-            rr[b].reshape(chunk, half_f),
+            rr[b],
             (((0,), (0,)), ((), ())),
             preferred_element_type=f32,
         )
 
     both[...] = acc[...].astype(bf).reshape(both.shape)
-    last = remote(both.at[1 - c], out.at[c], u_s.at[0], u_r.at[0], me.sibling())
-    mine = pltpu.make_async_copy(both.at[c], out.at[c], u_l.at[0])
+    there = out.at[:, cols(half_f, c)]
+    last = remote(both.at[1 - c], there, u_s.at[0], u_r.at[0], me.sibling())
+    mine = pltpu.make_async_copy(both.at[c], there, u_l.at[0])
     last.start()
     mine.start()
 
     @pl.loop(0, nz)
     def _(b):
         for buf, sem in ((sb, p_s), (ret, r_s)):
-            pltpu.make_async_copy(
-                buf.at[b, pl.ds(0, plane - 1)], buf.at[b, pl.ds(0, plane - 1)], sem.at[b]
-            ).wait()
+            wait_used(buf.at[b, pl.ds(0, plane - 1)], sem.at[b])
         swap(b).wait_send()
 
         @pl.when(b != z)
@@ -417,9 +462,7 @@
     def _(j):
         hidden_hop(j).wait_send()
 
-    pltpu.make_async_copy(
-        hsend.at[pl.ds(0, plane - 1)], hsend.at[pl.ds(0, plane - 1)], hp_s.at[0]
-    ).wait()
+    wait_used(hsend.at[pl.ds(0, plane - 1)], hp_s.at[0])
     for op in give:
         op.wait_send()
 
@@ -440,6 +483,7 @@
     n_routes, f = hs.shape
     half_d, half_f = d // 2, f // 2
     chunk = plane * BLK
+    few = plane * 2 * CAP
     dma = pltpu.SemaphoreType.DMA
     any_ = pl.BlockSpec(memory_space=pl.ANY)
     bf, f32 = jnp.bfloat16, jnp.float32
@@ -447,12 +491,13 @@
     w_rows = min(256, half_f)
     f_rows = min(256, half_f)
     vm = pltpu.VMEM
+    spans = len(SPANS)
     return pl.pallas_call(
         functools.partial(kernel, groups, members),
         name="exchange",
         out_shape=(
             jax.ShapeDtypeStruct((f, half_d), bf),
-            jax.ShapeDtypeStruct((2, n_routes, half_f), bf),
+            jax.ShapeDtypeStruct((n_routes, f), bf),
         ),
         in_specs=[any_] * 4,
         out_specs=(any_,) * 2,
@@ -465,23 +510,25 @@
             vm((2 * n_routes, half_f), bf),
             vm((plane, nz, BLK, half_f), bf),
             vm((plane, nz, BLK, half_f), bf),
-            vm((2, nz, plane, BLK, half_f), bf),
+            vm((nz, few, half_f), bf),
+            vm((2, nz, few, half_f), bf),
             vm((f_rows, nz * chunk), bf),
             vm((nz, 2, chunk, half_f), f32),
             vm((nz, chunk, half_f), f32),
             vm((nz, plane, BLK, half_f), bf),
             vm((nz, plane, BLK, half_f), bf),
-            vm((nz, plane, BLK, half_f), bf),
+            vm((nz, few, half_f), bf),
+            vm((nz, few, half_f), bf),
             vm((2 * n_routes, half_f), f32),
             vm((2, n_routes, half_f), bf),
             dma((3,)), dma((3,)), dma((3,)),
             dma((2, steps, 2)), dma((2, steps, 2)), dma((2, steps, 2)), dma((2, steps, 2)),
-            dma((nz,)), dma((nz,)), dma((nz,)),
-            dma((1,)), dma((1,)), dma((1,)),
+            dma((nz, spans)), dma((nz, spans)), dma((nz,)),
+            dma((1, spans)), dma((1, spans)), dma((1,)),
             dma((nz,)), dma((nz,)), dma((1,)),
             dma((nz,)), dma((nz,)),
             dma((nz,)), dma((nz,)),
-            dma((nz,)), dma((nz,)), dma((nz,)),
+            dma((nz, spans)), dma((nz, spans)), dma((nz,)),
             dma((nz,)), dma((nz,)), dma((1,)),
             dma((1,)), dma((1,)), dma((1,)), dma((1,)), dma((f // f_rows,)),
         ],
@@ -505,7 +552,7 @@
     same = expert[None, :] == expert[:, None]
     rank = jnp.sum((same & earlier).astype(jnp.int32), axis=1)
     ex, ez, ey = expert // (nz * ny), (expert // ny) % nz, expert % ny
-    slot = (ez * plane + ex * ny + ey) * BLK + core * PAD + rank
+    slot = (ez * plane + ex * ny + ey) * BLK + core * CAP + rank
     sid = jnp.concatenate([slot.reshape(top, tok), jnp.full((top, tok), -1, jnp.int32)], axis=0)
 
     gate = gate_weight.astype(jnp.float32)
@@ -517,7 +564,7 @@
     weight_grad, back = exchange(groups, members, out_grad, hs, sid, weight)
     weight_grad = weight_grad.reshape(1, f, d // 2)
 
-    unscaled = jnp.transpose(back.reshape(2, top, tok, f // 2), (2, 1, 0, 3)).reshape(tok, top, f)
+    unscaled = jnp.transpose(back.reshape(top, tok, f), (1, 0, 2))
     wide = unscaled.astype(jnp.float32)
     hidden_grad = (gate[:, :, None] * wide).astype(jnp.bfloat16)
     gate_grad = jnp.sum(wide * hidden_act.astype(jnp.float32), axis=2)

time: 218 us -> 189 us (0.87); the launches traced: 214 us -> 188 us
  Pallas kernels: 192 us -> 172 us
  local copies, waits for them, and re-layouts: 13.9 us -> 7.44 us
    pallas_call x1, Pallas kernels: 192 us -> 172 us  [exchange(): pl.pallas_call(functools.partial(kernel, groups, members), name='exchange...]
    convert_element_type x2 -> x0, local copies, waits for them, and re-layouts: 6.44 us -> none  [local(): wide = unscaled.astype(jnp.float32)]
where the time goes in v3:
time: 189 us; the launch traced here: 188 us
  Pallas kernels  172 us (91%)
  other arithmetic  7.7 us (4%)
  local copies, waits for them, and re-layouts  7.44 us (4%)
    pallas_call x1, Pallas kernels, exchange(): pl.pallas_call(functools.partial(kernel, groups, members), name='exchange...  172 us
    unnamed x8, local copies, waits for them, and re-layouts  4.78 us

profile of v3, /device:TPU:5, one launch (start us, length us, event | category | flops | bytes accessed | tf_op | source)
XLA Modules:
  0.0 188.3 jit_solution(864899877125295035)
XLA Ops:
  0.6 1.0 convert_reduce_fusion
  1.6 0.7 fusion.11
  2.3 0.6 concatenate.3.sid
  2.9 0.8 copy.15
  3.7 0.0 copy-start.1
  3.7 1.7 fusion.3
  5.5 1.3 copy.16
  6.8 0.0 copy-done.1
  6.8 172.5 %exchange.1 = (bf16[1024,1792]{1,0:T(8,128)(2,1)}, bf16[512,1024]{1,0:T(8,128)(2,1)}) custom-call(bf16[128,3584]{1,0:T(8,128)(2,1)} %og.1, bf16[512,1024]{1,0:T(8,128)(2,1)} %bitcast.31, s32[8,128]{1,0:T(8,128)} %concatenate.3.sid, bf16[4,256,1792]{2,1,0:T(8,128)(2,1)} %bitcast.32), custom_call_target="tpu_custom_call" | custom-call | tf_op jit(solution)/shard_map/exchange/pallas_call | solution.py:495
  179.2 0.0 copy-start
  179.2 0.0 copy-start.2
  179.3 1.5 bitcast_convert_fusion
  180.8 0.0 copy-done
  180.8 0.0 copy-done.2
  180.8 2.7 %fusion.1 = (f32[128,4]{1,0:T(8,128)S(1)}, bf16[128,4,1024]{2,1,0:T(4,128)(2,1)}) fusion(bf16[128,4,1024]{2,1,0:T(4,128)(2,1)S(1)} %copy-done, f32[4,128,1024]{2,1,0:T(8,128)S(1)} %bitcast_convert_fusion, f32[128,4]{1,0:T(8,128)S(1)} %copy-done.2), kind=kLoop, calls=%fused_computation.3 | loop fusion | flops 2620928 | bytes 4198400 | tf_op jit(solution)/shard_map/reduce_sum | solution.py:570
  183.5 0.7 copy.18
  184.2 4.1 %copy.22 = bf16[1,1024,1792]{2,1,0:T(8,128)(2,1)} copy(bf16[1,1024,1792]{2,1,0:T(8,128)(2,1)} %bitcast.33) | data formatting | bytes 7340032
Async XLA Ops:
  3.7 3.0 %copy-start.1 = (f32[128,4]{1,0:T(8,128)}, f32[128,4]{1,0:T(8,128)S(1)}, u32[]{:S(2)}) copy-start(f32[128,4]{1,0:T(8,128)S(1)} %copy.15) | copy-start | bytes 6148
  179.2 1.6 copy-start
  179.2 1.6 copy-start.2
